TPU v7x, 512 devices: a whole 4x8x8 slice. The times are simulated.
512 devices in a mesh: row: 16 (over y_hi, z), col: 32 (over y_lo, x, core).
Axes of the slice: x: 4, y: 8 (y_hi: 2, y_lo: 4; y = y_hi * 4 + y_lo), z: 8, core: 2. Of those that a mesh axis runs over, the one named last changes fastest.
Arguments:
- features: bfloat16 [65536, 256], P(('col', 'row')), may hold values from -6 to 6
- weight: bfloat16 [256, 256], replicated, may hold values from -0.375 to 0.375
- bias: float32 [256], replicated, may hold values from -3 to 3
- grad_out: bfloat16 [65536, 256], P(('row', 'col')), may hold values from -6 to 6
- tile_rows: int32 [16, 32, 128], P('row', 'col'), may hold values from 0 to 31
- tile_cols: int32 [16, 32, 128], P('row', 'col'), may hold values from 0 to 15
- tile_counts: int32 [16, 32], P('row', 'col'), may hold values from 1 to 128, as said below
- tile_values: bfloat16 [16, 32, 128, 128, 128], P('row', 'col'), may hold values from 0 to 0.011962891
Outputs:
- output: bfloat16 [65536, 256], P(('row', 'col'))
- grad_features: bfloat16 [65536, 256], P(('col', 'row'))
- grad_weight: float32 [256, 256], replicated
- grad_bias: float32 [256], replicated
Inputs may be any that keep to these rules, and one draw needn't show every extreme that they name: `tile_counts`: some grid cell has all 128 slots live. Tile coordinates may repeat within a cell; repeated tiles add.
All inputs are finite; a program needn't handle non-finite values.
Results may differ from a plain program's by a relative error of at most 0.018.
Values may be sent and summed in bfloat16 or wider, within the bound.
No kernel may reach another device: no remote copies, remote signals or barrier semaphores. Data moves between devices by JAX's collectives and lax.ppermute only.
A program may use at most 64 MiB of HBM per device.

v0:
```python
import jax
import jax.numpy as jnp
from jax import lax
from jax.sharding import PartitionSpec as P

GROUP = 8


def elu_value(pre):
    return jnp.where(pre > 0, pre, jnp.expm1(jnp.minimum(pre, 0.0)))


def elu_slope(pre):
    return jnp.where(pre > 0, jnp.float32(1.0), jnp.exp(jnp.minimum(pre, 0.0)))


def accumulate(values, dest_idx, src_idx, live, source, dest_tiles, transpose):
    side = values.shape[-1]
    width = source.shape[-1]
    group_size = GROUP
    blocks_all = source.reshape(source.shape[0] // side, side, width)

    def one_group(step, acc):
        first = step * group_size
        part_values = lax.dynamic_slice_in_dim(values, first, group_size, 0)
        part_dest = lax.dynamic_slice_in_dim(dest_idx, first, group_size, 0)
        part_src = lax.dynamic_slice_in_dim(src_idx, first, group_size, 0)
        blocks = jnp.take(blocks_all, part_src, axis=0)
        if transpose:
            prod = jnp.einsum(
                "gab,gac->gbc", part_values, blocks, preferred_element_type=jnp.float32
            )
        else:
            prod = jnp.einsum(
                "gab,gbc->gac", part_values, blocks, preferred_element_type=jnp.float32
            )
        keep = (jnp.arange(group_size) + first < live).astype(jnp.float32)
        return acc.at[part_dest].add(prod * keep[:, None, None])

    start_acc = jnp.zeros((dest_tiles, side, width), jnp.float32)
    steps_used = values.shape[0] // group_size
    total = lax.fori_loop(0, steps_used, one_group, start_acc)
    return total.reshape(dest_tiles * side, width)


def body(features, weight, bias, grad_out, tile_rows, tile_cols, tile_counts, tile_values):
    values = tile_values[0, 0]
    rows_idx = tile_rows[0, 0]
    cols_idx = tile_cols[0, 0]
    live = tile_counts[0, 0]
    side = values.shape[-1]
    share = features.shape[0]
    row_tiles = share * lax.axis_size("col") // side
    col_tiles = share * lax.axis_size("row") // side
    mixed = jnp.dot(features, weight, preferred_element_type=jnp.float32).astype(jnp.bfloat16)
    column_block = lax.all_gather(mixed, "row", axis=0, tiled=True)
    partial_value = accumulate(values, rows_idx, cols_idx, live, column_block, row_tiles, False)
    pre_share = (
        lax.psum_scatter(
            partial_value.astype(jnp.bfloat16), "col", scatter_dimension=0, tiled=True
        ).astype(jnp.float32)
        + bias[None, :]
    )
    grad_share = (grad_out.astype(jnp.float32) * elu_slope(pre_share)).astype(jnp.bfloat16)
    grad_block = lax.all_gather(grad_share, "col", axis=0, tiled=True)
    output = elu_value(pre_share).astype(jnp.bfloat16)
    back = accumulate(values, cols_idx, rows_idx, live, grad_block, col_tiles, True)
    grad_mixed = lax.psum_scatter(back.astype(jnp.bfloat16), "row", scatter_dimension=0, tiled=True)
    grad_features = lax.dot_general(
        grad_mixed, weight, (((1,), (1,)), ((), ())), preferred_element_type=jnp.float32
    ).astype(jnp.bfloat16)
    weight_term = lax.dot_general(
        features, grad_mixed, (((0,), (0,)), ((), ())), preferred_element_type=jnp.float32
    )
    bias_term = jnp.sum(grad_share.astype(jnp.float32), axis=0)
    grad_weight, grad_bias = lax.psum((weight_term, bias_term), ("row", "col"))
    return (output, grad_features, grad_weight, grad_bias)


def solution(mesh):
    placed = (
        P(("col", "row"), None),
        P(),
        P(),
        P(("row", "col"), None),
        P("row", "col", None),
        P("row", "col", None),
        P("row", "col"),
        P("row", "col", None, None, None),
    )
    return jax.shard_map(
        body,
        mesh=mesh,
        in_specs=placed,
        out_specs=(P(("row", "col"), None), P(("col", "row"), None), P(), P()),
        check_vma=False,
    )
```

profile of v0, /device:TPU:23, one launch (start us, length us, event | category | flops | bytes accessed | tf_op | source)
XLA Modules:
  0.0 1037.7 jit_solution(1046019565683276147)
XLA Ops:
  9.8 93.5 %all-gather.3.cloned.1.call-done = bf16[2048,256]{1,0:T(8,128)(2,1)} async-done(((bf16[128,256]{1,0:T(8,128)(2,1)}), bf16[2048,256]{1,0:T(8,128)(2,1)}) %all-gather.3.cloned.1.call-update) | async-done | bytes 1048592 | tf_op jit(solution)/shard_map/all_gather | solution.py:56
  105.7 96.6 %while.26 = (s32[]{:T(128)}, f32[32,128,256]{2,1,0:T(8,128)}, s32[128]{0:T(128)S(1)}, bf16[128,128,128]{2,1,0:T(8,128)(2,1)}, s32[128]{0:T(128)S(1)}, /*index=5*...) while((s32[]{:T(128)}, f32[32,128,256]{2,1,0:T(8,128)}, ...), condition=%wide.region_2.3_spmd, body=%wide.region_0.2_spmd.sunk | while | flops 67896424 | bytes 6033887 | solution.py:42
  108.4 3.3 scatter_fusion
  114.5 3.3 scatter_fusion
  120.6 3.3 scatter_fusion
  126.6 3.3 scatter_fusion
  138.6 3.3 scatter_fusion
  150.6 3.3 scatter_fusion
  162.7 3.3 scatter_fusion
  168.7 3.3 scatter_fusion
  174.7 3.3 scatter_fusion
  186.8 3.4 scatter_fusion
  192.9 3.4 scatter_fusion
  199.0 3.3 scatter_fusion
  202.3 3.8 convert_element_type.56
  206.2 125.6 %reduce-scatter.3.cloned.1.call-done = bf16[128,256]{1,0:T(8,128)(2,1)} async-done(((bf16[4096,256]{1,0:T(8,128)(2,1)}), bf16[128,256]{1,0:T(8,128)(2,1)}) %reduce-scatter.3.cloned.1.call-update) | async-done | bytes 65552 | tf_op jit(solution)/shard_map/reduce_scatter | solution.py:59
  333.5 6.4 copy.12
  339.9 75.5 %all-gather.5.cloned.1.call-done = bf16[4096,256]{1,0:T(8,128)(2,1)} async-done(((bf16[128,256]{1,0:T(8,128)(2,1)}), bf16[4096,256]{1,0:T(8,128)(2,1)}) %all-gather.5.cloned.1.call-update) | async-done | bytes 2097168 | tf_op jit(solution)/shard_map/all_gather | solution.py:65
  417.0 121.8 %while.27 = (s32[]{:T(128)}, f32[16,128,256]{2,1,0:T(8,128)}, s32[128]{0:T(128)S(1)}, bf16[128,128,128]{1,2,0:T(8,128)(2,1)}, s32[128]{0:T(128)S(1)}, /*index=5*...) while((s32[]{:T(128)}, f32[16,128,256]{2,1,0:T(8,128)}, ...), condition=%wide.region_6.7_spmd, body=%wide.region_4.6_spmd.sunk | while | flops 67896424 | bytes 6033887 | solution.py:42
  421.3 3.3 scatter_fusion.1
  428.9 3.3 scatter_fusion.1
  436.6 3.3 scatter_fusion.1
  444.2 3.3 scatter_fusion.1
  459.4 3.3 scatter_fusion.1
  474.6 3.3 scatter_fusion.1
  489.9 3.3 scatter_fusion.1
  505.1 3.3 scatter_fusion.1
  520.3 3.3 scatter_fusion.1
  527.9 3.3 scatter_fusion.1
  541.6 97.9 %psum.15 = f32[256]{0:T(256)} all-reduce(f32[256]{0:T(256)S(1)} %get-tuple-element.297), channel_id=1, replica_groups=mesh['row'=16,'col'=32] {'row','col'}, use_global_device_ids=true, to_apply=%region_10.11 | all-reduce | flops 256 | bytes 2048 | tf_op jit(solution)/shard_map/psum | solution.py:76
  639.5 113.2 %reduce-scatter.5.cloned.1.call-done = bf16[128,256]{1,0:T(8,128)(2,1)} async-done(((bf16[2048,256]{1,0:T(8,128)(2,1)}), bf16[128,256]{1,0:T(8,128)(2,1)}) %reduce-scatter.5.cloned.1.call-update) | async-done | bytes 65552 | tf_op jit(solution)/shard_map/reduce_scatter | solution.py:68
  756.2 273.2 %all-reduce.2.cloned.1.call-done = f32[256,256]{0,1:T(8,128)} async-done(((f32[256,256]{0,1:T(8,128)}), f32[256,256]{0,1:T(8,128)}) %all-reduce.2.cloned.1.call-update) | async-done | bytes 262160 | tf_op jit(solution)/shard_map/psum | solution.py:76
  (202 shorter events, 161.1 us)
Async XLA Ops:
  7.2 0.9 copy-start
  7.2 98.5 %copy-start.4 = (s32[1,1,128]{2,1,0:T(1,128)S(1)}, s32[1,1,128]{2,1,0:T(1,128)}, u32[]{:S(2)}) copy-start(s32[1,1,128]{2,1,0:T(1,128)} %param.16) | copy-start | bytes 1540
  7.2 98.5 %copy-start.5 = (s32[1,1,128]{2,1,0:T(1,128)S(1)}, s32[1,1,128]{2,1,0:T(1,128)}, u32[]{:S(2)}) copy-start(s32[1,1,128]{2,1,0:T(1,128)} %param.17) | copy-start | bytes 1540
  7.2 96.1 %all-gather.3.cloned.1.call-start = ((), (), s32[]{:S(2)}) async-start(), calls=%async_computation.2 | async-start | bytes 1114112 | tf_op jit(solution)/shard_map/all_gather | solution.py:56
  9.7 322.1 %reduce-scatter.3.cloned.1.call-start = ((), (), s32[]{:S(2)}) async-start(), calls=%async_computation.3 | async-start | bytes 2162688 | tf_op jit(solution)/shard_map/reduce_scatter | solution.py:59
  103.3 2.4 copy-start.1
  202.3 129.6 %copy-start.3 = (bf16[128,256]{1,0:T(8,128)(2,1)S(1)}, bf16[128,256]{1,0:T(8,128)(2,1)}, u32[]{:S(2)}) copy-start(bf16[128,256]{1,0:T(8,128)(2,1)} %param.15) | copy-start | bytes 196612
  202.3 129.6 %copy-start.6 = (f32[256]{0:T(256)S(1)}, f32[256]{0:T(256)}, u32[]{:S(2)}) copy-start(f32[256]{0:T(256)} %param.14) | copy-start | bytes 3076
  206.1 209.3 %all-gather.5.cloned.1.call-start = ((), (), s32[]{:S(2)}) async-start(), calls=%async_computation.4 | async-start | bytes 2162688 | tf_op jit(solution)/shard_map/all_gather | solution.py:65
  333.4 419.3 %reduce-scatter.5.cloned.1.call-start = ((), (), s32[]{:S(2)}) async-start(), calls=%async_computation.5 | async-start | bytes 1114112 | tf_op jit(solution)/shard_map/reduce_scatter | solution.py:68
  538.8 213.9 %copy-start.2 = (bf16[128,256]{1,0:T(8,128)(2,1)S(1)}, bf16[128,256]{1,0:T(8,128)(2,1)}, u32[]{:S(2)}) copy-start(bf16[128,256]{1,0:T(8,128)(2,1)} %param.12) | copy-start | bytes 196612
  541.6 487.8 %all-reduce.2.cloned.1.call-start = ((), (), s32[]{:S(2)}) async-start(), calls=%async_computation.6 | async-start | bytes 524288 | tf_op jit(solution)/shard_map/psum | solution.py:76
Sparse Core Ops, SparseCore 0:
  11.8 91.4 all-gather.2
  206.3 125.5 reduce-scatter.2
  334.8 80.5 all-gather.4
  541.7 210.9 reduce-scatter.4
  758.9 270.4 all-reduce.1
where the time goes:
time: 1040 us
  waiting for transfers between devices  681 us (65%)
  other arithmetic  140 us (13%)
  blocking collectives  97.9 us (9%)
  local copies, waits for them, and re-layouts  57 us (5%)
  matrix products  47.3 us (5%)
  between operations  13.8 us (1%)
    psum x1, waiting for transfers between devices, body(): grad_weight, grad_bias = lax.psum((weight_term, bias_term), ('row', 'col'))  273 us
    reduce_scatter x1, waiting for transfers between devices, body(): lax.psum_scatter(partial_value.astype(jnp.bfloat16), 'col', scatter_dimen...  126 us
    reduce_scatter x1, waiting for transfers between devices, body(): lax.psum_scatter(back.astype(jnp.bfloat16), 'row', scatter_dimension=0, t...  113 us
    scatter-add x32, other arithmetic, one_group(): return acc.at[part_dest].add(prod * keep[:, None, None])  106 us
    psum x1, blocking collectives, body(): grad_weight, grad_bias = lax.psum((weight_term, bias_term), ('row', 'col'))  97.9 us
    all_gather x1, waiting for transfers between devices, body(): column_block = lax.all_gather(mixed, 'row', axis=0, tiled=True)  93.5 us
    all_gather x1, waiting for transfers between devices, body(): grad_block = lax.all_gather(grad_share, 'col', axis=0, tiled=True)  75.5 us
    gather x32, local copies, waits for them, and re-layouts, one_group(): blocks = jnp.take(blocks_all, part_src, axis=0)  44 us
  transfers between devices with their start and end apart: 5, of which 5 were waited for; matrix products, arithmetic and copies ran while one was open for 1% of the time, Pallas kernels for 0%

commit v1 on v0

--- a/solution.py
+++ b/solution.py
@@ -53,7 +53,9 @@
     row_tiles = share * lax.axis_size("col") // side
     col_tiles = share * lax.axis_size("row") // side
     mixed = jnp.dot(features, weight, preferred_element_type=jnp.float32).astype(jnp.bfloat16)
-    column_block = lax.all_gather(mixed, "row", axis=0, tiled=True)
+    column_block = jnp.concatenate(
+        lax.all_to_all(jnp.stack([mixed] * lax.axis_size("row")), "row", 0, 0), axis=0
+    )
     partial_value = accumulate(values, rows_idx, cols_idx, live, column_block, row_tiles, False)
     pre_share = (
         lax.psum_scatter(

time: 1040 us -> 993 us (0.955)
  waiting for transfers between devices: 681 us -> 619 us
  starting transfers between devices: 0.21 us -> 13.8 us
    all_gather x1 -> x0, waiting for transfers between devices: 93.5 us -> none  [body(): column_block = lax.all_gather(mixed, 'row', axis=0, tiled=True)]
    all_to_all x0 -> x1, waiting for transfers between devices: none -> 30.6 us  [body(): lax.all_to_all(jnp.stack([mixed] * lax.axis_size('row')), 'row', 0, 0)]
    all_to_all x0 -> x1, starting transfers between devices: none -> 13.6 us  [body(): lax.all_to_all(jnp.stack([mixed] * lax.axis_size('row')), 'row', 0, 0)]
where the time goes in v1:
time: 993 us; the launch traced here: 989 us
  waiting for transfers between devices  619 us (62%)
  other arithmetic  140 us (14%)
  blocking collectives  97.8 us (10%)
  local copies, waits for them, and re-layouts  58.1 us (6%)
  matrix products  46.7 us (5%)
  starting transfers between devices  13.8 us (1%)
  between operations  13.8 us (1%)
    psum x1, waiting for transfers between devices, body(): grad_weight, grad_bias = lax.psum((weight_term, bias_term), ('row', 'col'))  273 us
    reduce_scatter x1, waiting for transfers between devices, body(): lax.psum_scatter(partial_value.astype(jnp.bfloat16), 'col', scatter_dimen...  127 us
    reduce_scatter x1, waiting for transfers between devices, body(): lax.psum_scatter(back.astype(jnp.bfloat16), 'row', scatter_dimension=0, t...  113 us
    scatter-add x32, other arithmetic, one_group(): return acc.at[part_dest].add(prod * keep[:, None, None])  105 us
    psum x1, blocking collectives, body(): grad_weight, grad_bias = lax.psum((weight_term, bias_term), ('row', 'col'))  97.8 us
    all_gather x1, waiting for transfers between devices, body(): grad_block = lax.all_gather(grad_share, 'col', axis=0, tiled=True)  75.5 us
    gather x32, local copies, waits for them, and re-layouts, one_group(): blocks = jnp.take(blocks_all, part_src, axis=0)  44 us
    all_to_all x1, waiting for transfers between devices, body(): lax.all_to_all(jnp.stack([mixed] * lax.axis_size('row')), 'row', 0, 0)  30.6 us
  transfers between devices with their start and end apart: 5, of which 5 were waited for; matrix products, arithmetic and copies ran while one was open for 1% of the time, Pallas kernels for 0%

profile of v1, /device:TPU:23, one launch (start us, length us, event | category | flops | bytes accessed | tf_op | source)
XLA Modules:
  0.0 989.4 jit_solution(15930878396133804536)
XLA Ops:
  10.2 13.6 %all-to-all-start = ((bf16[16,128,256]{2,1,0:T(8,128)(2,1)}), bf16[16,128,256]{2,1,0:T(8,128)(2,1)S(1)}, u32[]{:S(2)}, u32[]{:S(2)}) async-start(bf16[16,128,256]{2,1,0:T(8,128)(2,1)} %stack.2), calls=%async_computation | async-start | bytes 2097152 | tf_op jit(solution)/shard_map/all_to_all | solution.py:57
  23.8 30.6 %all-to-all-done = bf16[16,128,256]{2,1,0:T(8,128)(2,1)S(1)} async-done(((bf16[16,128,256]{2,1,0:T(8,128)(2,1)}), bf16[16,128,256]{2,1,0:T(8,128)(2,1)S(1)}, u32[]{:S(2)}, u32[]{:S(2)}) %all-to-all-start) | async-done | bytes 1048608 | tf_op jit(solution)/shard_map/all_to_all | solution.py:57
  56.8 96.4 %while.26 = (s32[]{:T(128)}, f32[32,128,256]{2,1,0:T(8,128)}, s32[128]{0:T(128)S(1)}, bf16[128,128,128]{2,1,0:T(8,128)(2,1)}, s32[128]{0:T(128)S(1)}, /*index=5*...) while((s32[]{:T(128)}, f32[32,128,256]{2,1,0:T(8,128)}, ...), condition=%wide.region_2.3_spmd, body=%wide.region_0.2_spmd.sunk | while | flops 67896424 | bytes 6033887 | solution.py:42
  59.5 3.3 scatter_fusion
  65.5 3.4 scatter_fusion
  71.6 3.3 scatter_fusion
  77.7 3.3 scatter_fusion
  101.7 3.3 scatter_fusion
  113.7 3.3 scatter_fusion
  119.8 3.3 scatter_fusion
  125.8 3.4 scatter_fusion
  143.9 3.3 scatter_fusion
  149.9 3.3 scatter_fusion
  153.2 3.8 convert_element_type.56
  157.2 126.7 %reduce-scatter.3.cloned.1.call-done = bf16[128,256]{1,0:T(8,128)(2,1)} async-done(((bf16[4096,256]{1,0:T(8,128)(2,1)}), bf16[128,256]{1,0:T(8,128)(2,1)}) %reduce-scatter.3.cloned.1.call-update) | async-done | bytes 65552 | tf_op jit(solution)/shard_map/reduce_scatter | solution.py:61
  285.5 6.4 copy.12
  291.8 75.5 %all-gather.2.cloned.1.call-done = bf16[4096,256]{1,0:T(8,128)(2,1)} async-done(((bf16[128,256]{1,0:T(8,128)(2,1)}), bf16[4096,256]{1,0:T(8,128)(2,1)}) %all-gather.2.cloned.1.call-update) | async-done | bytes 2097168 | tf_op jit(solution)/shard_map/all_gather | solution.py:67
  368.9 121.9 %while.27 = (s32[]{:T(128)}, f32[16,128,256]{2,1,0:T(8,128)}, s32[128]{0:T(128)S(1)}, bf16[128,128,128]{1,2,0:T(8,128)(2,1)}, s32[128]{0:T(128)S(1)}, /*index=5*...) while((s32[]{:T(128)}, f32[16,128,256]{2,1,0:T(8,128)}, ...), condition=%wide.region_6.7_spmd, body=%wide.region_4.6_spmd.sunk | while | flops 67896424 | bytes 6033887 | solution.py:42
  373.2 3.3 scatter_fusion.1
  380.9 3.4 scatter_fusion.1
  388.6 3.3 scatter_fusion.1
  396.2 3.3 scatter_fusion.1
  411.4 3.3 scatter_fusion.1
  426.6 3.3 scatter_fusion.1
  441.8 3.3 scatter_fusion.1
  464.6 3.3 scatter_fusion.1
  472.3 3.3 scatter_fusion.1
  479.9 3.3 scatter_fusion.1
  487.5 3.3 scatter_fusion.1
  493.6 97.8 %psum.15 = f32[256]{0:T(256)} all-reduce(f32[256]{0:T(256)S(1)} %get-tuple-element.297), channel_id=1, replica_groups=mesh['row'=16,'col'=32] {'row','col'}, use_global_device_ids=true, to_apply=%region_10.11 | all-reduce | flops 256 | bytes 2048 | tf_op jit(solution)/shard_map/psum | solution.py:78
  591.4 113.3 %reduce-scatter.5.cloned.1.call-done = bf16[128,256]{1,0:T(8,128)(2,1)} async-done(((bf16[2048,256]{1,0:T(8,128)(2,1)}), bf16[128,256]{1,0:T(8,128)(2,1)}) %reduce-scatter.5.cloned.1.call-update) | async-done | bytes 65552 | tf_op jit(solution)/shard_map/reduce_scatter | solution.py:70
  708.1 273.0 %all-reduce.2.cloned.1.call-done = f32[256,256]{0,1:T(8,128)} async-done(((f32[256,256]{0,1:T(8,128)}), f32[256,256]{0,1:T(8,128)}) %all-reduce.2.cloned.1.call-update) | async-done | bytes 262160 | tf_op jit(solution)/shard_map/psum | solution.py:78
  (200 shorter events, 164.8 us)
Async XLA Ops:
  7.2 0.9 copy-start
  7.2 49.6 %copy-start.3 = (s32[1,1,128]{2,1,0:T(1,128)S(1)}, s32[1,1,128]{2,1,0:T(1,128)}, u32[]{:S(2)}) copy-start(s32[1,1,128]{2,1,0:T(1,128)} %param.16) | copy-start | bytes 1540
  7.2 49.6 %copy-start.4 = (s32[1,1,128]{2,1,0:T(1,128)S(1)}, s32[1,1,128]{2,1,0:T(1,128)}, u32[]{:S(2)}) copy-start(s32[1,1,128]{2,1,0:T(1,128)} %param.17) | copy-start | bytes 1540
  10.2 44.2 %all-to-all-start = ((bf16[16,128,256]{2,1,0:T(8,128)(2,1)}), bf16[16,128,256]{2,1,0:T(8,128)(2,1)S(1)}, u32[]{:S(2)}, u32[]{:S(2)}) async-start(bf16[16,128,256]{2,1,0:T(8,128)(2,1)} %stack.2), calls=%async_computation | async-start | bytes 2097152 | tf_op jit(solution)/shard_map/all_to_all | solution.py:57
  23.8 260.1 %reduce-scatter.3.cloned.1.call-start = ((), (), s32[]{:S(2)}) async-start(), calls=%async_computation.3 | async-start | bytes 2162688 | tf_op jit(solution)/shard_map/reduce_scatter | solution.py:61
  153.2 130.6 %copy-start.2 = (bf16[128,256]{1,0:T(8,128)(2,1)S(1)}, bf16[128,256]{1,0:T(8,128)(2,1)}, u32[]{:S(2)}) copy-start(bf16[128,256]{1,0:T(8,128)(2,1)} %param.15) | copy-start | bytes 196612
  153.2 130.6 %copy-start.5 = (f32[256]{0:T(256)S(1)}, f32[256]{0:T(256)}, u32[]{:S(2)}) copy-start(f32[256]{0:T(256)} %param.14) | copy-start | bytes 3076
  157.1 210.3 %all-gather.2.cloned.1.call-start = ((), (), s32[]{:S(2)}) async-start(), calls=%async_computation.4 | async-start | bytes 2162688 | tf_op jit(solution)/shard_map/all_gather | solution.py:67
  285.4 419.2 %reduce-scatter.5.cloned.1.call-start = ((), (), s32[]{:S(2)}) async-start(), calls=%async_computation.5 | async-start | bytes 1114112 | tf_op jit(solution)/shard_map/reduce_scatter | solution.py:70
  490.8 213.9 %copy-start.1 = (bf16[128,256]{1,0:T(8,128)(2,1)S(1)}, bf16[128,256]{1,0:T(8,128)(2,1)}, u32[]{:S(2)}) copy-start(bf16[128,256]{1,0:T(8,128)(2,1)} %param.12) | copy-start | bytes 196612
  493.5 487.6 %all-reduce.2.cloned.1.call-start = ((), (), s32[]{:S(2)}) async-start(), calls=%async_computation.6 | async-start | bytes 524288 | tf_op jit(solution)/shard_map/psum | solution.py:78
Sparse Core Ops, SparseCore 0:
  157.2 126.5 reduce-scatter.2
  286.8 80.5 all-gather.1
  493.6 210.9 reduce-scatter.4
  710.8 270.2 all-reduce.1
